TPU v7x, 32 devices: a whole 2x2x4 slice. The times are simulated.
32 devices in a mesh: row: 4 (over x, core), col: 2 (over y), depth: 4 (over z).
Axes of the slice: x: 2, y: 2, z: 4, core: 2. Of those that a mesh axis runs over, the one named last changes fastest.
Arguments:
- tokens: bfloat16 [64, 6144], P(('col', 'depth'), 'row'), may hold values from -6 to 6
- first_weight: bfloat16 [6144, 24576], P('row', ('col', 'depth')), may hold values from -0.078125 to 0.078125
- first_tangent: bfloat16 [6144, 24576], P('row', ('col', 'depth')), may hold values from -0.078125 to 0.078125
- second_weight: bfloat16 [24576, 6144], P(('col', 'depth'), 'row'), may hold values from -0.0390625 to 0.0390625
- second_tangent: bfloat16 [24576, 6144], P(('col', 'depth'), 'row'), may hold values from -0.0390625 to 0.0390625
Outputs:
- grad_first: float32 [6144, 24576], P('row', ('col', 'depth'))
- grad_second: float32 [24576, 6144], P(('col', 'depth'), 'row')
All inputs are finite; a program needn't handle non-finite values.
Results may differ from a plain program's by a relative error of at most 0.0047.
Values may be sent and summed in bfloat16 or wider, within the bound.
A program may use at most 192 MiB of HBM per device.

v0:
```python
import math
import jax
import jax.numpy as jnp
from jax import lax
from jax.sharding import PartitionSpec as P


def gelu_parts(hidden, hidden_tan):
    inner = 0.7978845608 * (hidden + 0.044715 * hidden * hidden * hidden)
    tval = jnp.tanh(inner)
    active = (0.5 * hidden * (1.0 + tval)).astype(jnp.bfloat16)
    slopes = 0.5 * (1.0 + tval) + 0.5 * hidden * (1.0 - tval * tval) * 0.7978845608 * (
        1.0 + 3.0 * 0.044715 * hidden * hidden
    )
    active_tan = (slopes * hidden_tan).astype(jnp.bfloat16)
    return (active, active_tan, slopes)


def on_device(tokens, first_weight, first_tangent, second_weight, second_tangent):
    gathered = lax.all_gather(tokens, ("col", "depth"), axis=0, tiled=True)
    hidden = jnp.dot(gathered, first_weight, preferred_element_type=jnp.float32)
    hidden_tan = jnp.dot(gathered, first_tangent, preferred_element_type=jnp.float32)
    hidden, hidden_tan = lax.psum((hidden, hidden_tan), "row")
    active, active_tan, slopes = gelu_parts(hidden, hidden_tan)
    partial_value = jnp.dot(
        active_tan, second_weight, preferred_element_type=jnp.float32
    ) + jnp.dot(active, second_tangent, preferred_element_type=jnp.float32)
    out_tan = lax.psum(partial_value, ("col", "depth")).astype(jnp.bfloat16)
    backward = lax.dot_general(
        out_tan, second_weight, (((1,), (1,)), ((), ())), preferred_element_type=jnp.float32
    )
    backward = lax.psum(backward, "row")
    back_hidden = (backward * slopes).astype(jnp.bfloat16)
    factor = 1.0 / math.sqrt(gathered.shape[0])
    grad_second = (
        lax.dot_general(
            active, out_tan, (((0,), (0,)), ((), ())), preferred_element_type=jnp.float32
        )
        * factor
    )
    grad_first = (
        lax.dot_general(
            gathered, back_hidden, (((0,), (0,)), ((), ())), preferred_element_type=jnp.float32
        )
        * factor
    )
    return (grad_first, grad_second)


def solution(mesh):
    return jax.shard_map(
        on_device,
        mesh=mesh,
        in_specs=(
            P(("col", "depth"), "row"),
            P("row", ("col", "depth")),
            P("row", ("col", "depth")),
            P(("col", "depth"), "row"),
            P(("col", "depth"), "row"),
        ),
        out_specs=(P("row", ("col", "depth")), P(("col", "depth"), "row")),
        check_vma=False,
    )
```

profile of v0, /device:TPU:0, one launch (start us, length us, event | category | flops | bytes accessed | tf_op | source)
XLA Modules:
  0.0 220.9 jit_solution(1123703977794834401)
XLA Ops:
  7.2 0.0 slice-start.3
  7.2 0.0 all-reduce.7.cloned.1.call-start
  7.2 33.1 %all_gather.3 = bf16[64,1536]{1,0:T(8,128)(2,1)S(1)} all-gather(bf16[8,1536]{1,0:T(8,128)(2,1)} %param.5), channel_id=1, replica_groups=mesh['row'=4,'col'=2,'depth'=4] {'col','depth'}, dimensions={0}, use_global_device_ids=true | all-gather | bytes 221184 | tf_op jit(solution)/shard_map/all_gather | solution.py:20
  40.3 0.0 slice-start.4
  40.3 0.0 slice-start.5
  40.3 6.5 %fusion.12 = f32[64,3072]{1,0:T(8,128)} fusion(bf16[64,1536]{1,0:T(8,128)(2,1)S(1)} %all_gather.3, bf16[1536,3072]{1,0:T(8,128)(2,1)} %param.7), kind=kOutput, calls=%fused_computation.18 | convolution fusion | flops 603979776 | bytes 10420224 | tf_op jit(solution)/shard_map/dot_general | solution.py:22
  46.8 0.0 slice-done.3
  46.8 0.0 slice-done.4
  46.8 0.0 slice-done.5
  46.8 2.6 %fusion.11 = f32[64,3072]{1,0:T(8,128)} fusion(bf16[64,1536]{1,0:T(8,128)(2,1)S(1)} %all_gather.3, bf16[1536,3072]{1,0:T(8,128)(2,1)S(1)} %bitcast.15), kind=kOutput, calls=%fused_computation.17 | convolution fusion | flops 603979776 | bytes 10420224 | tf_op jit(solution)/shard_map/dot_general | solution.py:21
  49.4 0.0 slice-start
  49.4 0.0 all-reduce.7.cloned.1.call-update
  49.5 0.0 all-reduce.5.cloned.1.call-start
  49.5 44.0 %all-reduce.7.cloned.1.call-done = (f32[64,3072]{1,0:T(8,128)}, f32[64,3072]{1,0:T(8,128)}) async-done(((f32[64,3072]{1,0:T(8,128)}, f32[64,3072]{1,0:T(8,128)}), (f32[64,3072]{1,0:T(8,128)}, f32[64,3072]{1,0:T(8,128)})) %all-reduce.7.cloned.1.call-update) | async-done | bytes 1572880 | tf_op jit(solution)/shard_map/psum | solution.py:23
  93.5 0.0 slice-start.1
  93.5 0.0 slice-start.2
  93.5 0.0 copy-start
  93.5 6.3 %fusion.5 = f32[64,1536]{1,0:T(8,128)S(1)} fusion(bf16[3072,1536]{1,0:T(8,128)(2,1)} %param.8, f32[64,3072]{1,0:T(8,128)} %get-tuple-element.4, f32[64,3072]{1,0:T(8,128)} %get-tuple-element.5), kind=kOutput, calls=%fused_computation.13 | convolution fusion | flops 607715328 | bytes 11403264 | tf_op jit(solution)/shard_map/dot_general | solution.py:25
  99.8 0.0 slice-done
  99.8 0.0 slice-done.1
  99.8 0.3 slice-done.2
  100.1 0.1 copy-done
  100.2 1.8 convolution_add_fusion
  102.0 44.5 %all-reduce.8 = bf16[64,1536]{1,0:T(8,128)(2,1)S(1)} all-reduce(f32[64,1536]{1,0:T(8,128)S(1)} %convolution_add_fusion), channel_id=1, replica_groups=mesh['row'=4,'col'=2,'depth'=4] {'col','depth'}, use_global_device_ids=true, to_apply=%region_2.0 | all-reduce | flops 98304 | bytes 589824 | tf_op jit(solution)/shard_map/psum | solution.py:28
  146.5 7.5 %fusion.13 = f32[64,3072]{1,0:T(8,128)} fusion(bf16[64,1536]{1,0:T(8,128)(2,1)S(1)} %all-reduce.8, bf16[3072,1536]{1,0:T(8,128)(2,1)} %param.8), kind=kOutput, calls=%fused_computation.19 | convolution fusion | flops 603979776 | bytes 10420224 | tf_op jit(solution)/shard_map/dot_general | solution.py:29
  154.0 0.0 all-reduce.5.cloned.1.call-update
  154.0 8.3 %convolution_multiply_fusion = f32[3072,1536]{1,0:T(8,128)} fusion(bf16[64,1536]{1,0:T(8,128)(2,1)S(1)} %all-reduce.8, f32[64,3072]{1,0:T(8,128)S(1)} %copy-done), kind=kOutput, calls=%fused_computation.1 | convolution fusion | flops 610467840 | bytes 19857408 | tf_op jit(solution)/shard_map/dot_general | solution.py:36
  162.3 23.6 %all-reduce.5.cloned.1.call-done = f32[64,3072]{1,0:T(8,128)} async-done(((f32[64,3072]{1,0:T(8,128)}), f32[64,3072]{1,0:T(8,128)}) %all-reduce.5.cloned.1.call-update) | async-done | bytes 786448 | tf_op jit(solution)/shard_map/psum | solution.py:32
  185.9 9.6 %multiply_bitcast_fusion = f32[1536,3072]{0,1:T(8,128)} fusion(bf16[64,1536]{1,0:T(8,128)(2,1)S(1)} %all_gather.3, f32[64,3072]{1,0:T(8,128)} %all-reduce.5.cloned.1.call-done, f32[64,3072]{1,0:T(8,128)S(1)} %copy-done), kind=kOutput, calls=%fused_computation | convolution fusion | flops 612433920 | bytes 20643840 | tf_op jit(solution)/shard_map/dot_general | solution.py:42
  195.4 18.6 %copy.7 = f32[1536,3072]{1,0:T(8,128)} copy(f32[1536,3072]{0,1:T(8,128)} %multiply_bitcast_fusion) | data formatting | bytes 37748736
  (2 shorter events, 0.0 us)
Async XLA Ops:
  7.2 39.6 %slice-start.3 = ((s8[9437184]{0:T(1024)(128)(4,1)}), s8[1048576]{0:T(1024)(128)(4,1)S(1)}, s32[]{:S(2)}) async-start(s8[9437184]{0:T(1024)(128)(4,1)} %bitcast.14), calls=%async_computation.5 | async-start | bytes 2097152
  7.2 86.3 %all-reduce.7.cloned.1.call-start = ((), (), s32[]{:S(2)}) async-start(), calls=%async_computation.1 | async-start | bytes 3145728 | tf_op jit(solution)/shard_map/psum | solution.py:23
  40.3 6.5 %slice-start.4 = ((s8[9437184]{0:T(1024)(128)(4,1)}), s8[4194304]{0:T(1024)(128)(4,1)S(1)}, s32[]{:S(2)}) async-start(s8[9437184]{0:T(1024)(128)(4,1)} %bitcast.14), calls=%async_computation.6 | async-start | bytes 8388608
  40.3 6.5 %slice-start.5 = ((s8[9437184]{0:T(1024)(128)(4,1)}), s8[4194304]{0:T(1024)(128)(4,1)S(1)}, s32[]{:S(2)}) async-start(s8[9437184]{0:T(1024)(128)(4,1)} %bitcast.14), calls=%async_computation.7 | async-start | bytes 8388608
  49.4 50.3 %slice-start = ((s8[9437184]{0:T(1024)(128)(4,1)}), s8[1048576]{0:T(1024)(128)(4,1)S(1)}, s32[]{:S(2)}) async-start(s8[9437184]{0:T(1024)(128)(4,1)} %bitcast.12), calls=%async_computation.2 | async-start | bytes 2097152
  49.5 136.4 %all-reduce.5.cloned.1.call-start = ((), (), s32[]{:S(2)}) async-start(), calls=%async_computation | async-start | bytes 1572864 | tf_op jit(solution)/shard_map/psum | solution.py:32
  93.5 6.3 %slice-start.1 = ((s8[9437184]{0:T(1024)(128)(4,1)}), s8[4194304]{0:T(1024)(128)(4,1)S(1)}, s32[]{:S(2)}) async-start(s8[9437184]{0:T(1024)(128)(4,1)} %bitcast.12), calls=%async_computation.3 | async-start | bytes 8388608
  93.5 6.6 %slice-start.2 = ((s8[9437184]{0:T(1024)(128)(4,1)}), s8[4194304]{0:T(1024)(128)(4,1)S(1)}, s32[]{:S(2)}) async-start(s8[9437184]{0:T(1024)(128)(4,1)} %bitcast.12), calls=%async_computation.4 | async-start | bytes 8388608
  93.5 6.7 %copy-start = (f32[64,3072]{1,0:T(8,128)S(1)}, f32[64,3072]{1,0:T(8,128)}, u32[]{:S(2)}) copy-start(f32[64,3072]{1,0:T(8,128)} %get-tuple-element.5) | copy-start | bytes 2359300
Sparse Core Ops, SparseCore 0:
  49.6 43.8 all-reduce.6
  154.1 31.7 all-reduce.4
where the time goes:
time: 221 us
  blocking collectives  77.6 us (35%)
  waiting for transfers between devices  67.6 us (31%)
  matrix products  42.5 us (19%)
  local copies, waits for them, and re-layouts  19.1 us (9%)
  between operations  14.1 us (6%)
    psum x1, blocking collectives, on_device(): out_tan = lax.psum(partial_value, ('col', 'depth')).astype(jnp.bfloat16)  44.5 us
    psum x1, waiting for transfers between devices, on_device(): hidden, hidden_tan = lax.psum((hidden, hidden_tan), 'row')  44 us
    all_gather x1, blocking collectives, on_device(): gathered = lax.all_gather(tokens, ('col', 'depth'), axis=0, tiled=True)  33.1 us
    psum x1, waiting for transfers between devices, on_device(): backward = lax.psum(backward, 'row')  23.6 us
    unnamed x15, local copies, waits for them, and re-layouts  19.1 us
    dot_general x1, matrix products, on_device(): lax.dot_general(gathered, back_hidden, (((0,), (0,)), ((), ())), preferre...  9.56 us
    dot_general x1, matrix products, on_device(): lax.dot_general(active, out_tan, (((0,), (0,)), ((), ())), preferred_elem...  8.3 us
    dot_general x1, matrix products, on_device(): lax.dot_general(out_tan, second_weight, (((1,), (1,)), ((), ())), preferr...  7.5 us
  transfers between devices with their start and end apart: 2, of which 2 were waited for; matrix products, arithmetic and copies ran while one was open for 4% of the time, Pallas kernels for 0%

commit v1 on v0

--- a/solution.py
+++ b/solution.py
@@ -3,6 +3,16 @@
 import jax.numpy as jnp
 from jax import lax
 from jax.sharding import PartitionSpec as P
+
+
+def guide_stocks_on_mesh(work_x, which_axis):
+    lanes = jax.lax.axis_size(which_axis)
+    block_out, y_new = (work_x, 0)
+    while 1 << y_new < lanes:
+        n_now = jax.lax.ppermute(block_out, which_axis, [(w, w ^ 1 << y_new) for w in range(lanes)])
+        block_out = block_out + n_now
+        y_new = y_new + 1
+    return block_out
 
 
 def gelu_parts(hidden, hidden_tan):
@@ -29,7 +39,7 @@
     backward = lax.dot_general(
         out_tan, second_weight, (((1,), (1,)), ((), ())), preferred_element_type=jnp.float32
     )
-    backward = lax.psum(backward, "row")
+    backward = guide_stocks_on_mesh(backward, "row")
     back_hidden = (backward * slopes).astype(jnp.bfloat16)
     factor = 1.0 / math.sqrt(gathered.shape[0])
     grad_second = (

time: 221 us -> 209 us (0.946)
  waiting for transfers between devices: 67.6 us -> 57 us
  matrix products: 42.5 us -> 39.9 us
    psum x1 -> x0, waiting for transfers between devices: 23.6 us -> none  [on_device(): backward = lax.psum(backward, 'row')]
    ppermute x0 -> x2, waiting for transfers between devices: none -> 12.9 us  [guide_stocks_on_mesh(): jax.lax.ppermute(block_out, which_axis, [(w, w ^ 1 << y_new) for w in ran...]
  transfers between devices with their start and end apart: 2 -> 3, of which waited for: 2 -> 3; matrix products, arithmetic and copies ran while one was open for 4% -> 4% of each run, Pallas kernels for 0% -> 0%
where the time goes in v1:
time: 209 us
  blocking collectives  77.6 us (37%)
  waiting for transfers between devices  57 us (27%)
  matrix products  39.9 us (19%)
  local copies, waits for them, and re-layouts  19.1 us (9%)
  between operations  14.1 us (7%)
    psum x1, blocking collectives, on_device(): out_tan = lax.psum(partial_value, ('col', 'depth')).astype(jnp.bfloat16)  44.5 us
    psum x1, waiting for transfers between devices, on_device(): hidden, hidden_tan = lax.psum((hidden, hidden_tan), 'row')  44 us
    all_gather x1, blocking collectives, on_device(): gathered = lax.all_gather(tokens, ('col', 'depth'), axis=0, tiled=True)  33.1 us
    unnamed x15, local copies, waits for them, and re-layouts  19.1 us
    ppermute x2, waiting for transfers between devices, guide_stocks_on_mesh(): jax.lax.ppermute(block_out, which_axis, [(w, w ^ 1 << y_new) for w in ran...  12.9 us
    dot_general x1, matrix products, on_device(): lax.dot_general(active, out_tan, (((0,), (0,)), ((), ())), preferred_elem...  8.28 us
    dot_general x1, matrix products, on_device(): lax.dot_general(gathered, back_hidden, (((0,), (0,)), ((), ())), preferre...  7.91 us
    dot_general x1, matrix products, on_device(): lax.dot_general(out_tan, second_weight, (((1,), (1,)), ((), ())), preferr...  6.61 us
  transfers between devices with their start and end apart: 3, of which 3 were waited for; matrix products, arithmetic and copies ran while one was open for 4% of the time, Pallas kernels for 0%

profile of v1, /device:TPU:0, one launch (start us, length us, event | category | flops | bytes accessed | tf_op | source)
XLA Modules:
  0.0 208.6 jit_solution(10201613922126537078)
XLA Ops:
  7.2 0.0 slice-start.3
  7.2 0.0 all-reduce.4.cloned.1.call-start
  7.2 33.1 %all_gather.3 = bf16[64,1536]{1,0:T(8,128)(2,1)S(1)} all-gather(bf16[8,1536]{1,0:T(8,128)(2,1)} %param.5), channel_id=1, replica_groups=mesh['row'=4,'col'=2,'depth'=4] {'col','depth'}, dimensions={0}, use_global_device_ids=true | all-gather | bytes 221184 | tf_op jit(solution)/shard_map/all_gather | solution.py:30
  40.3 0.0 slice-start.4
  40.3 0.0 slice-start.5
  40.3 6.5 %fusion.12 = f32[64,3072]{1,0:T(8,128)} fusion(bf16[64,1536]{1,0:T(8,128)(2,1)S(1)} %all_gather.3, bf16[1536,3072]{1,0:T(8,128)(2,1)} %param.7), kind=kOutput, calls=%fused_computation.18 | convolution fusion | flops 603979776 | bytes 10420224 | tf_op jit(solution)/shard_map/dot_general | solution.py:32
  46.8 0.0 slice-done.3
  46.8 0.0 slice-done.4
  46.8 0.0 slice-done.5
  46.8 2.6 %fusion.11 = f32[64,3072]{1,0:T(8,128)} fusion(bf16[64,1536]{1,0:T(8,128)(2,1)S(1)} %all_gather.3, bf16[1536,3072]{1,0:T(8,128)(2,1)S(1)} %bitcast.15), kind=kOutput, calls=%fused_computation.17 | convolution fusion | flops 603979776 | bytes 10420224 | tf_op jit(solution)/shard_map/dot_general | solution.py:31
  49.4 0.0 slice-start
  49.4 0.0 all-reduce.4.cloned.1.call-update
  49.5 44.0 %all-reduce.4.cloned.1.call-done = (f32[64,3072]{1,0:T(8,128)}, f32[64,3072]{1,0:T(8,128)}) async-done(((f32[64,3072]{1,0:T(8,128)}, f32[64,3072]{1,0:T(8,128)}), (f32[64,3072]{1,0:T(8,128)}, f32[64,3072]{1,0:T(8,128)})) %all-reduce.4.cloned.1.call-update) | async-done | bytes 1572880 | tf_op jit(solution)/shard_map/psum | solution.py:33
  93.5 0.0 slice-start.1
  93.5 0.0 slice-start.2
  93.5 0.0 copy-start
  93.5 6.3 %fusion.5 = f32[64,1536]{1,0:T(8,128)S(1)} fusion(bf16[3072,1536]{1,0:T(8,128)(2,1)} %param.8, f32[64,3072]{1,0:T(8,128)} %get-tuple-element.4, f32[64,3072]{1,0:T(8,128)} %get-tuple-element.5), kind=kOutput, calls=%fused_computation.13 | convolution fusion | flops 607715328 | bytes 11403264 | tf_op jit(solution)/shard_map/dot_general | solution.py:35
  99.8 0.0 slice-done
  99.8 0.0 slice-done.1
  99.8 0.3 slice-done.2
  100.1 0.1 copy-done
  100.2 1.8 convolution_add_fusion
  102.0 44.5 %all-reduce.5 = bf16[64,1536]{1,0:T(8,128)(2,1)S(1)} all-reduce(f32[64,1536]{1,0:T(8,128)S(1)} %convolution_add_fusion), channel_id=1, replica_groups=mesh['row'=4,'col'=2,'depth'=4] {'col','depth'}, use_global_device_ids=true, to_apply=%region_2.0 | all-reduce | flops 98304 | bytes 589824 | tf_op jit(solution)/shard_map/psum | solution.py:38
  146.5 6.6 %fusion.13 = f32[64,3072]{1,0:T(8,128)S(1)} fusion(bf16[64,1536]{1,0:T(8,128)(2,1)S(1)} %all-reduce.5, bf16[3072,1536]{1,0:T(8,128)(2,1)} %param.8), kind=kOutput, calls=%fused_computation.19 | convolution fusion | flops 603979776 | bytes 10420224 | tf_op jit(solution)/shard_map/dot_general | solution.py:39
  153.1 0.1 collective-permute-start
  153.2 2.3 %collective-permute-done = f32[64,3072]{1,0:T(8,128)S(1)} collective-permute-done((f32[64,3072]{1,0:T(8,128)S(1)}, f32[64,3072]{1,0:T(8,128)S(1)}, u32[]{:S(2)}, u32[]{:S(2)}) %collective-permute-start) | collective-permute-done | bytes 786464 | tf_op jit(solution)/shard_map/ppermute | solution.py:12
  155.5 0.1 add.33
  155.5 0.7 collective-permute-start.1
  156.3 8.3 %convolution_multiply_fusion = f32[3072,1536]{1,0:T(8,128)} fusion(bf16[64,1536]{1,0:T(8,128)(2,1)S(1)} %all-reduce.5, f32[64,3072]{1,0:T(8,128)S(1)} %copy-done), kind=kOutput, calls=%fused_computation.1 | convolution fusion | flops 610467840 | bytes 19857408 | tf_op jit(solution)/shard_map/dot_general | solution.py:46
  164.6 10.6 %collective-permute-done.1 = f32[64,3072]{1,0:T(8,128)S(1)} collective-permute-done((f32[64,3072]{1,0:T(8,128)S(1)}, f32[64,3072]{1,0:T(8,128)S(1)}, u32[]{:S(2)}, u32[]{:S(2)}) %collective-permute-start.1) | collective-permute-done | bytes 786464 | tf_op jit(solution)/shard_map/ppermute | solution.py:12
  175.2 7.9 %multiply_bitcast_fusion = f32[1536,3072]{0,1:T(8,128)} fusion(bf16[64,1536]{1,0:T(8,128)(2,1)S(1)} %all_gather.3, f32[64,3072]{1,0:T(8,128)S(1)} %add.33, f32[64,3072]{1,0:T(8,128)S(1)} %collective-permute-done.1, f32[64,3072]{1,0:T(8,128)S(1)} %copy-done), kind=kOutput, calls=%fused_computation | convolution fusion | flops 612630528 | bytes 21430272 | tf_op jit(solution)/shard_map/dot_general | solution.py:52
  183.1 18.6 %copy.7 = f32[1536,3072]{1,0:T(8,128)} copy(f32[1536,3072]{0,1:T(8,128)} %multiply_bitcast_fusion) | data formatting | bytes 37748736
  (2 shorter events, 0.0 us)
Async XLA Ops:
  7.2 39.6 %slice-start.3 = ((s8[9437184]{0:T(1024)(128)(4,1)}), s8[1048576]{0:T(1024)(128)(4,1)S(1)}, s32[]{:S(2)}) async-start(s8[9437184]{0:T(1024)(128)(4,1)} %bitcast.14), calls=%async_computation.4 | async-start | bytes 2097152
  7.2 86.3 %all-reduce.4.cloned.1.call-start = ((), (), s32[]{:S(2)}) async-start(), calls=%async_computation | async-start | bytes 3145728 | tf_op jit(solution)/shard_map/psum | solution.py:33
  40.3 6.5 %slice-start.4 = ((s8[9437184]{0:T(1024)(128)(4,1)}), s8[4194304]{0:T(1024)(128)(4,1)S(1)}, s32[]{:S(2)}) async-start(s8[9437184]{0:T(1024)(128)(4,1)} %bitcast.14), calls=%async_computation.5 | async-start | bytes 8388608
  40.3 6.5 %slice-start.5 = ((s8[9437184]{0:T(1024)(128)(4,1)}), s8[4194304]{0:T(1024)(128)(4,1)S(1)}, s32[]{:S(2)}) async-start(s8[9437184]{0:T(1024)(128)(4,1)} %bitcast.14), calls=%async_computation.6 | async-start | bytes 8388608
  49.4 50.3 %slice-start = ((s8[9437184]{0:T(1024)(128)(4,1)}), s8[1048576]{0:T(1024)(128)(4,1)S(1)}, s32[]{:S(2)}) async-start(s8[9437184]{0:T(1024)(128)(4,1)} %bitcast.12), calls=%async_computation.1 | async-start | bytes 2097152
  93.5 6.3 %slice-start.1 = ((s8[9437184]{0:T(1024)(128)(4,1)}), s8[4194304]{0:T(1024)(128)(4,1)S(1)}, s32[]{:S(2)}) async-start(s8[9437184]{0:T(1024)(128)(4,1)} %bitcast.12), calls=%async_computation.2 | async-start | bytes 8388608
  93.5 6.6 %slice-start.2 = ((s8[9437184]{0:T(1024)(128)(4,1)}), s8[4194304]{0:T(1024)(128)(4,1)S(1)}, s32[]{:S(2)}) async-start(s8[9437184]{0:T(1024)(128)(4,1)} %bitcast.12), calls=%async_computation.3 | async-start | bytes 8388608
  93.5 6.7 %copy-start = (f32[64,3072]{1,0:T(8,128)S(1)}, f32[64,3072]{1,0:T(8,128)}, u32[]{:S(2)}) copy-start(f32[64,3072]{1,0:T(8,128)} %get-tuple-element.5) | copy-start | bytes 2359300
  153.1 2.4 %collective-permute-start = (f32[64,3072]{1,0:T(8,128)S(1)}, f32[64,3072]{1,0:T(8,128)S(1)}, u32[]{:S(2)}, u32[]{:S(2)}) collective-permute-start(f32[64,3072]{1,0:T(8,128)S(1)} %fusion.13), channel_id=1, source_target_pairs={{0,8},{8,0},{16,24},{24,16},{1,9},{9,1},{17,25},{25,17},{2,10},{10... | collective-permute-start | bytes 2359304 | tf_op jit(solution)/shard_map/ppermute | solution.py:12
  155.5 19.6 %collective-permute-start.1 = (f32[64,3072]{1,0:T(8,128)S(1)}, f32[64,3072]{1,0:T(8,128)S(1)}, u32[]{:S(2)}, u32[]{:S(2)}) collective-permute-start(f32[64,3072]{1,0:T(8,128)S(1)} %add.33), channel_id=1, source_target_pairs={{0,16},{8,24},{16,0},{24,8},{1,17},{9,25},{17,1},{25,9},{2,18},{10... | collective-permute-start | bytes 2359304 | tf_op jit(solution)/shard_map/ppermute | solution.py:12
Sparse Core Ops, SparseCore 0:
  49.6 43.8 all-reduce.3
